TPU v7x, 32 devices: a whole 2x2x4 slice. The times are simulated.
32 devices in a mesh: narrow: 2 (over x), wide: 16 (over z, y, core).
Axes of the slice: x: 2, y: 2, z: 4, core: 2. Of those that a mesh axis runs over, the one named last changes fastest.
Arguments:
- patches: bfloat16 [64, 256, 1152], P(('narrow', 'wide')), may hold values from -6 to 6
- condition: float32 [64, 1152], P(('narrow', 'wide')), may hold values from -6 to 6
- image_counts: int32 [32], P(('narrow', 'wide')), may hold values from 1 to 2, as said below
- ada_weight: bfloat16 [1152, 6912], P(None, 'wide'), may hold values from -0.1875 to 0.1875
- ada_bias: bfloat16 [6912], P('wide'), may hold values from -3 to 3
- inproj_weight: bfloat16 [1152, 3456], P('wide'), may hold values from -0.1875 to 0.1875
- inproj_bias: bfloat16 [2304], P('wide'), may hold values from -2 to 2
- outproj_weight: bfloat16 [1152, 1152], P('wide'), may hold values from -0.75 to 0.75
- outproj_bias: bfloat16 [1152], P('wide'), may hold values from -2 to 2
- up_weight: bfloat16 [1152, 4608], P('wide'), may hold values from -0.1875 to 0.1875
- up_bias: bfloat16 [4608], P('wide'), may hold values from -3 to 3
- down_weight: bfloat16 [4608, 1152], P('wide'), may hold values from -0.09375 to 0.09375
- down_bias: bfloat16 [1152], P('wide'), may hold values from -2 to 2
- cotangent: bfloat16 [64, 256, 1152], P(('narrow', 'wide')), may hold values from -6 to 6
Outputs:
- output: bfloat16 [64, 256, 1152], P(('narrow', 'wide'))
- grad_patches: bfloat16 [64, 256, 1152], P(('narrow', 'wide'))
- grad_condition: float32 [64, 1152], P(('narrow', 'wide'))
- grad_ada_weight: float32 [1152, 6912], P(None, 'wide')
- grad_ada_bias: float32 [6912], P('wide')
- grad_inproj_weight: float32 [1152, 3456], P('wide')
- grad_inproj_bias: float32 [2304], P('wide')
- grad_outproj_weight: float32 [1152, 1152], P('wide')
- grad_outproj_bias: float32 [1152], P('wide')
- grad_up_weight: float32 [1152, 4608], P('wide')
- grad_up_bias: float32 [4608], P('wide')
- grad_down_weight: float32 [4608, 1152], P('wide')
- grad_down_bias: float32 [1152], P('wide')
Inputs may be any that keep to these rules, and one draw needn't show every extreme that they name: `image_counts`: each device's number of live image slots; a device's live slots are its first ones. In every draw some device has 2 and some device has 1.
All inputs are finite; a program needn't handle non-finite values.
Results may differ from a plain program's by a relative error of at most 0.02.
The roundings to bfloat16 on the way count: a program that leaves them out, or rounds other values in their place, can miss the bound.
Values may be sent and summed in bfloat16 or wider, within the bound.
A program may use at most 192 MiB of HBM per device.

v0:
```python
from functools import partial
import jax
import jax.numpy as jnp
from jax import lax
from jax.sharding import PartitionSpec as P

HEADS = 16
norm_eps = 1e-06


def normalize(values):
    center = jnp.mean(values, axis=-1, keepdims=True)
    shifted = values - center
    inv_std = lax.rsqrt(jnp.mean(shifted * shifted, axis=-1, keepdims=True) + norm_eps)
    return (shifted * inv_std, inv_std)


def normalize_reverse(normed, inv_std, grad_normed):
    mean_grad = jnp.mean(grad_normed, axis=-1, keepdims=True)
    mean_proj = jnp.mean(grad_normed * normed, axis=-1, keepdims=True)
    return inv_std * (grad_normed - mean_grad - normed * mean_proj)


def matmul_rows(left, right):
    return jnp.dot(left, right, preferred_element_type=jnp.float32)


def matmul_back(left, right):
    return lax.dot_general(
        left, right, (((1,), (1,)), ((), ())), preferred_element_type=jnp.float32
    )


def matmul_outer(left, right):
    return lax.dot_general(
        left, right, (((0,), (0,)), ((), ())), preferred_element_type=jnp.float32
    )


def block_term(factors, count, first, width):
    pieces = []
    for left, right, base in factors:
        lower = max(first, base)
        upper = min(first + width, base + right.shape[1])
        if lower < upper:
            rows_part = lax.slice_in_dim(left, 0, count, axis=1)
            pieces.append(matmul_outer(rows_part, right[:, lower - base : upper - base]))
    return jnp.concatenate(pieces, axis=1)


def per_device(
    patches,
    condition,
    image_counts,
    ada_weight,
    ada_bias,
    inproj_weight,
    inproj_bias,
    outproj_weight,
    outproj_bias,
    up_weight,
    up_bias,
    down_weight,
    down_bias,
    cotangent,
):
    slots, seq_len, model_width = patches.shape
    head_dim = model_width // HEADS
    scale_qk = head_dim ** (-0.5)
    row_total = slots * seq_len
    wide_count = lax.axis_size("wide")
    live = (jnp.arange(slots) < image_counts[0]).astype(jnp.float32)[:, None, None]
    cond_act = jax.nn.silu(condition).astype(jnp.bfloat16)
    cond_all = lax.all_gather(cond_act, "wide", axis=0, tiled=True)
    mod_part = (matmul_rows(cond_all, ada_weight) + ada_bias.astype(jnp.float32)).astype(
        jnp.bfloat16
    )
    modulation = lax.all_to_all(mod_part, "wide", split_axis=0, concat_axis=1, tiled=True).astype(
        jnp.float32
    )
    segment_list = [
        modulation[:, None, number * model_width : (number + 1) * model_width]
        for number in range(6)
    ]
    (
        selfattn_offset,
        selfattn_scale,
        selfattn_gate,
        perceptron_offset,
        perceptron_scale,
        perceptron_gate,
    ) = segment_list
    fetched = (
        lax.all_gather(inproj_weight, "wide", axis=0, tiled=True),
        lax.all_gather(inproj_bias, "wide", axis=0, tiled=True),
        lax.all_gather(outproj_weight, "wide", axis=0, tiled=True),
        lax.all_gather(outproj_bias, "wide", axis=0, tiled=True),
        lax.all_gather(up_weight, "wide", axis=0, tiled=True),
        lax.all_gather(up_bias, "wide", axis=0, tiled=True),
        lax.all_gather(down_weight, "wide", axis=0, tiled=True),
        lax.all_gather(down_bias, "wide", axis=0, tiled=True),
    )
    w_inproj, b_inproj, w_outproj, b_outproj, w_up, b_up, w_down, b_down = fetched
    input_rows = patches.astype(jnp.float32)
    normalized_first, inverse_deviation = normalize(input_rows)
    first_input = (
        (normalized_first * (1.0 + selfattn_scale) + selfattn_offset)
        .astype(jnp.bfloat16)
        .reshape(row_total, model_width)
    )
    proj_bias = b_inproj.astype(jnp.float32)
    full_bias = jnp.concatenate(
        [proj_bias[:model_width], jnp.zeros((model_width,), jnp.float32), proj_bias[model_width:]]
    )
    projected = (matmul_rows(first_input, w_inproj) + full_bias).astype(jnp.bfloat16)
    query_rows = projected[:, :model_width].reshape(slots, seq_len, HEADS, head_dim)
    key_rows = projected[:, model_width : 2 * model_width].reshape(slots, seq_len, HEADS, head_dim)
    value_rows = projected[:, 2 * model_width :].reshape(slots, seq_len, HEADS, head_dim)
    scores = (
        jnp.einsum("sqhe,skhe->shqk", query_rows, key_rows, preferred_element_type=jnp.float32)
        * scale_qk
    )
    log_total = jax.nn.logsumexp(scores, axis=-1, keepdims=True)
    probs = jnp.exp(scores - log_total).astype(jnp.bfloat16)
    attended = jnp.einsum("shqk,skhe->sqhe", probs, value_rows, preferred_element_type=jnp.float32)
    attended = attended.astype(jnp.bfloat16).reshape(row_total, model_width)
    residual_branch = (matmul_rows(attended, w_outproj) + b_outproj.astype(jnp.float32)).reshape(
        slots, seq_len, model_width
    )
    between_state = input_rows + selfattn_gate * residual_branch
    normed_b, inv_b = normalize(between_state)
    second_in = (
        (normed_b * (1.0 + perceptron_scale) + perceptron_offset)
        .astype(jnp.bfloat16)
        .reshape(row_total, model_width)
    )
    hidden = matmul_rows(second_in, w_up) + b_up.astype(jnp.float32)
    gelu_value, gelu_pull = jax.vjp(partial(jax.nn.gelu, approximate=True), hidden)
    activated = gelu_value.astype(jnp.bfloat16)
    mlp_out = (matmul_rows(activated, w_down) + b_down.astype(jnp.float32)).reshape(
        slots, seq_len, model_width
    )
    output = ((between_state + perceptron_gate * mlp_out) * live).astype(jnp.bfloat16)
    back_weights = (
        lax.all_gather(inproj_weight, "wide", axis=0, tiled=True),
        lax.all_gather(inproj_bias, "wide", axis=0, tiled=True),
        lax.all_gather(outproj_weight, "wide", axis=0, tiled=True),
        lax.all_gather(outproj_bias, "wide", axis=0, tiled=True),
        lax.all_gather(up_weight, "wide", axis=0, tiled=True),
        lax.all_gather(up_bias, "wide", axis=0, tiled=True),
        lax.all_gather(down_weight, "wide", axis=0, tiled=True),
        lax.all_gather(down_bias, "wide", axis=0, tiled=True),
    )
    wb_inproj, _, wb_outproj, _, wb_up, _, wb_down, _ = back_weights
    grad_out = cotangent.astype(jnp.float32) * live
    grad_gate_mlp = jnp.sum(grad_out * mlp_out, axis=1)
    grad_mlp = (grad_out * perceptron_gate).astype(jnp.bfloat16).reshape(row_total, model_width)
    grad_down_bias = jnp.sum(grad_mlp.astype(jnp.float32), axis=0)
    grad_act = matmul_back(grad_mlp, wb_down)
    grad_hidden = gelu_pull(grad_act)[0].astype(jnp.bfloat16)
    grad_up_bias = jnp.sum(grad_hidden.astype(jnp.float32), axis=0)
    grad_second = matmul_back(grad_hidden, wb_up).reshape(slots, seq_len, model_width)
    grad_scale_mlp = jnp.sum(grad_second * normed_b, axis=1)
    grad_shift_mlp = jnp.sum(grad_second, axis=1)
    between_gradient = grad_out + normalize_reverse(
        normed_b, inv_b, grad_second * (1.0 + perceptron_scale)
    )
    selfattn_gate_gradient = jnp.sum(between_gradient * residual_branch, axis=1)
    residual_branch_gradient = (
        (between_gradient * selfattn_gate).astype(jnp.bfloat16).reshape(row_total, model_width)
    )
    grad_outproj_bias = jnp.sum(residual_branch_gradient.astype(jnp.float32), axis=0)
    grad_attended = (
        matmul_back(residual_branch_gradient, wb_outproj)
        .astype(jnp.bfloat16)
        .reshape(slots, seq_len, HEADS, head_dim)
    )
    scores_again = (
        jnp.einsum("sqhe,skhe->shqk", query_rows, key_rows, preferred_element_type=jnp.float32)
        * scale_qk
    )
    probs_full = jnp.exp(scores_again - log_total)
    grad_values = jnp.einsum(
        "shqk,sqhe->skhe",
        probs_full.astype(jnp.bfloat16),
        grad_attended,
        preferred_element_type=jnp.float32,
    )
    grad_probs = jnp.einsum(
        "sqhe,skhe->shqk", grad_attended, value_rows, preferred_element_type=jnp.float32
    )
    row_dot = jnp.sum(grad_probs * probs_full, axis=-1, keepdims=True)
    grad_scores = (probs_full * (grad_probs - row_dot)).astype(jnp.bfloat16)
    grad_queries = (
        jnp.einsum("shqk,skhe->sqhe", grad_scores, key_rows, preferred_element_type=jnp.float32)
        * scale_qk
    )
    grad_keys = (
        jnp.einsum("shqk,sqhe->skhe", grad_scores, query_rows, preferred_element_type=jnp.float32)
        * scale_qk
    )
    grad_projected = jnp.concatenate(
        [
            grad_queries.reshape(row_total, model_width),
            grad_keys.reshape(row_total, model_width),
            grad_values.reshape(row_total, model_width),
        ],
        axis=1,
    ).astype(jnp.bfloat16)
    proj_sums = jnp.sum(grad_projected.astype(jnp.float32), axis=0)
    grad_inproj_bias = jnp.concatenate([proj_sums[:model_width], proj_sums[2 * model_width :]])
    first_gradient = matmul_back(grad_projected, wb_inproj).reshape(slots, seq_len, model_width)
    selfattn_scale_gradient = jnp.sum(first_gradient * normalized_first, axis=1)
    selfattn_offset_gradient = jnp.sum(first_gradient, axis=1)
    grad_patches = (
        between_gradient
        + normalize_reverse(
            normalized_first, inverse_deviation, first_gradient * (1.0 + selfattn_scale)
        )
    ).astype(jnp.bfloat16)
    grad_modulation = jnp.concatenate(
        [
            selfattn_offset_gradient,
            selfattn_scale_gradient,
            selfattn_gate_gradient,
            grad_shift_mlp,
            grad_scale_mlp,
            grad_gate_mlp,
        ],
        axis=1,
    ).astype(jnp.bfloat16)
    grad_mod_part = lax.all_to_all(grad_modulation, "wide", split_axis=1, concat_axis=0, tiled=True)
    grad_ada_weight = matmul_outer(cond_all, grad_mod_part)
    grad_ada_bias = jnp.sum(grad_mod_part.astype(jnp.float32), axis=0)
    grad_cond_part = matmul_back(grad_mod_part, ada_weight)
    grad_cond_act = lax.psum_scatter(
        grad_cond_part.astype(jnp.bfloat16), "wide", scatter_dimension=0, tiled=True
    ).astype(jnp.float32)
    _, silu_pull = jax.vjp(jax.nn.silu, condition)
    grad_condition = silu_pull(grad_cond_act)[0]
    bias_shares = (
        lax.psum_scatter(
            grad_inproj_bias.astype(jnp.bfloat16), "wide", scatter_dimension=0, tiled=True
        ).astype(jnp.float32),
        lax.psum_scatter(
            grad_outproj_bias.astype(jnp.bfloat16), "wide", scatter_dimension=0, tiled=True
        ).astype(jnp.float32),
        lax.psum_scatter(
            grad_up_bias.astype(jnp.bfloat16), "wide", scatter_dimension=0, tiled=True
        ).astype(jnp.float32),
        lax.psum_scatter(
            grad_down_bias.astype(jnp.bfloat16), "wide", scatter_dimension=0, tiled=True
        ).astype(jnp.float32),
    )
    ff_width = activated.shape[1]
    input_factors = (
        (first_input, grad_projected, 0),
        (attended, residual_branch_gradient, 3 * model_width),
        (second_in, grad_hidden, 4 * model_width),
    )
    down_factors = ((activated, grad_mlp, 0),)
    input_block = (4 * model_width + ff_width) // 4
    down_block = model_width // 2
    block_jobs = [
        (input_factors, model_width, number * input_block, input_block) for number in range(4)
    ]
    block_jobs = block_jobs + [
        (down_factors, ff_width, number * down_block, down_block) for number in range(2)
    ]

    def reduce_block(factors, rows, first, width):
        return lax.psum_scatter(
            block_term(factors, lax.axis_size("wide") * (rows // wide_count), first, width).astype(
                jnp.bfloat16
            ),
            "wide",
            scatter_dimension=0,
            tiled=True,
        ).astype(jnp.float32)

    shards = [reduce_block(*job) for job in block_jobs]
    input_grads = jnp.concatenate(shards[:4], axis=1)
    grad_down_weight = jnp.concatenate(shards[4:], axis=1)
    summed = (
        lax.psum(grad_ada_weight.astype(jnp.bfloat16), "narrow").astype(jnp.float32),
        lax.psum(grad_ada_bias.astype(jnp.bfloat16), "narrow").astype(jnp.float32),
        lax.psum(input_grads[:, : 3 * model_width].astype(jnp.bfloat16), "narrow").astype(
            jnp.float32
        ),
        lax.psum(bias_shares[0].astype(jnp.bfloat16), "narrow").astype(jnp.float32),
        lax.psum(
            input_grads[:, 3 * model_width : 4 * model_width].astype(jnp.bfloat16), "narrow"
        ).astype(jnp.float32),
        lax.psum(bias_shares[1].astype(jnp.bfloat16), "narrow").astype(jnp.float32),
        lax.psum(input_grads[:, 4 * model_width :].astype(jnp.bfloat16), "narrow").astype(
            jnp.float32
        ),
        lax.psum(bias_shares[2].astype(jnp.bfloat16), "narrow").astype(jnp.float32),
        lax.psum(grad_down_weight.astype(jnp.bfloat16), "narrow").astype(jnp.float32),
        lax.psum(bias_shares[3].astype(jnp.bfloat16), "narrow").astype(jnp.float32),
    )
    return (
        output,
        grad_patches,
        grad_condition,
        summed[0],
        summed[1],
        summed[2],
        summed[3],
        summed[4],
        summed[5],
        summed[6],
        summed[7],
        summed[8],
        summed[9],
    )


def solution(mesh):
    in_specs = (
        P(("narrow", "wide"), None, None),
        P(("narrow", "wide"), None),
        P(("narrow", "wide")),
        P(None, "wide"),
        P("wide"),
        P("wide", None),
        P("wide"),
        P("wide", None),
        P("wide"),
        P("wide", None),
        P("wide"),
        P("wide", None),
        P("wide"),
        P(("narrow", "wide"), None, None),
    )
    out_specs = (
        P(("narrow", "wide"), None, None),
        P(("narrow", "wide"), None, None),
        P(("narrow", "wide"), None),
        P(None, "wide"),
        P("wide"),
        P("wide", None),
        P("wide"),
        P("wide", None),
        P("wide"),
        P("wide", None),
        P("wide"),
        P("wide", None),
        P("wide"),
    )
    return jax.shard_map(
        per_device, mesh=mesh, in_specs=in_specs, out_specs=out_specs, check_vma=False
    )
```

profile of v0, /device:TPU:0, one launch (start us, length us, event | category | flops | bytes accessed | tf_op | source)
XLA Modules:
  0.0 1013.1 jit_solution(17286262413155684345)
XLA Ops:
  10.9 23.9 %all-gather = bf16[16,2,1152]{2,1,0:T(2,128)(2,1)S(1)} all-gather(bf16[1,2,1152]{2,1,0:T(2,128)(2,1)S(1)} %fusion.42), channel_id=1, replica_groups=mesh['narrow'=2,'wide'=16] {'wide'}, dimensions={0}, use_global_device_ids=true | all-gather | bytes 78336 | tf_op jit(solution)/shard_map/all_gather | solution.py:74
  36.5 3.5 all-to-all-start
  44.1 64.5 %all-reduce.10 = (bf16[2304]{0:T(1024)(128)(2,1)S(1)}, bf16[1152]{0:T(1024)(128)(2,1)S(1)}, bf16[4608]{0:T(1024)(128)(2,1)S(1)}) all-reduce(bf16[2304]{0:T(1024)(128)(2,1)S(1)} %dynamic-update-slice, bf16[1152]{0:T(1024)(128)(2,1)S(1)} %dynamic-update-slice.1, ...), channel_id=1, replica_groups=mesh['narrow'=2,'wide'=16] {'wide'}, use_global_device_ids=true, to_apply=%add | all-reduce | flops 8064 | bytes 32256
  113.0 2.7 fusion.46
  116.3 8.9 add_convert_fusion
  127.1 5.0 reshape.221
  132.0 2.6 copy.93
  134.6 5.7 reshape.222
  140.4 3.1 copy.94
  143.5 4.7 reshape.220
  148.2 3.2 copy.95
  151.4 3.0 multiply_reduce_fusion.1
  160.9 4.1 convolution_add_fusion.1
  168.5 50.5 %all-gather.10.cloned.1.call-done = bf16[1152,4608]{1,0:T(8,128)(2,1)} async-done(((bf16[72,4608]{1,0:T(8,128)(2,1)}), bf16[1152,4608]{1,0:T(8,128)(2,1)}) %all-gather.10.cloned.1.call-update) | async-done | bytes 10616848 | tf_op jit(solution)/shard_map/all_gather | solution.py:98
  219.0 13.7 %multiply_convert_fusion = (bf16[512,4608]{1,0:T(8,128)(2,1)}, f32[512,4608]{1,0:T(8,128)}) fusion(f32[4608]{0:T(1024)S(1)} %copy-done.51, bf16[512,1152]{1,0:T(8,128)(2,1)} %bitcast.131, bf16[1152,4608]{1,0:T(8,128)(2,1)} %all-gather.10.cloned.1.call-done), kind=kOutput, calls=%fused_computation.12 | convolution fusion | flops 5459410944 | bytes 25970688 | tf_op jit(solution)/shard_map/dot_general | solution.py:25
  232.7 75.1 %all-gather.12.cloned.1.call-done = bf16[4608,1152]{1,0:T(8,128)(2,1)} async-done(((bf16[288,1152]{1,0:T(8,128)(2,1)}), bf16[4608,1152]{1,0:T(8,128)(2,1)}) %all-gather.12.cloned.1.call-update) | async-done | bytes 10616848 | tf_op jit(solution)/shard_map/all_gather | solution.py:100
  307.8 15.9 %fusion.47 = (bf16[4608]{0:T(1024)(128)(2,1)S(1)}, bf16[512,4608]{1,0:T(8,128)(2,1)S(1)}) fusion(f32[512,4608]{1,0:T(8,128)} %get-tuple-element.67, f32[4608]{0:T(1024)S(1)} %copy-done.51, bf16[512,1152]{1,0:T(8,128)(2,1)} %bitcast.125, bf16[4608,1152]{1,0:T(8,128)(2,1)} %all-gather.12.cloned.1.call-done), kind=kOutput, calls=%fused_computation.124 | convolution fusion | flops 5487717888 | bytes 25979904 | tf_op jit(solution)/shard_map/dot_general | solution.py:29
  323.7 2.2 copy-done.60
  325.9 5.0 convolution_convert_fusion.1
  331.0 7.4 convolution_convert_fusion
  338.5 13.8 %fusion.29 = (f32[512]{0:T(512)S(1)}, f32[512,1152]{1,0:T(8,128)}) fusion(f32[2,1152]{1,0:T(2,128)S(1)} %get-tuple-element.52, bf16[512,4608]{1,0:T(8,128)(2,1)} %copy-done.60, bf16[1152,4608]{1,0:T(8,128)(2,1)} %all-gather.10.cloned.1.call-done), kind=kOutput, calls=%fused_computation.56 | convolution fusion | flops 5436997120 | bytes 17705984 | tf_op jit(solution)/shard_map/dot_general | solution.py:29
  352.3 3.4 fusion.30
  360.4 2.9 convolution_convert_fusion.7
  363.3 5.7 reshape.223
  369.0 4.1 copy.99
  373.1 6.4 multiply_reduce_fusion
  379.6 4.8 multiply_convert_fusion.1
  390.6 5.9 convolution_convert_fusion.2
  396.8 5.4 fusion.32
  407.3 2.7 pad_maximum_fusion
  410.1 8.9 convolution_convert_fusion.4
  419.3 9.4 convolution_convert_fusion.3
  429.5 2.6 constant_dynamic-update-slice_fusion.2
  434.3 2.6 reduce.10
  436.9 61.5 %all-reduce.9 = (bf16[1152]{0:T(1024)(128)(2,1)S(1)}, bf16[2304]{0:T(1024)(128)(2,1)S(1)}, bf16[1152]{0:T(1024)(128)(2,1)S(1)}, bf16[4608]{0:T(1024)(128)(2,1)S(1)}, bf16[1152]{0:T(1024)(128)(2,1)S(1)}) all-reduce(bf16[1152]{0:T(1024)(128)(2,1)S(1)} %dynamic-update-slice.3, ...), channel_id=1, replica_groups=mesh['narrow'=2,'wide'=16] {'wide'}, use_global_device_ids=true, to_apply=%add.3 | all-reduce | flops 10368 | bytes 41472
  498.4 10.4 %fusion.28 = (f32[512]{0:T(512)S(1)}, f32[512,1152]{1,0:T(8,128)S(1)}) fusion(f32[2,1152]{1,0:T(2,128)S(1)} %copy-done.42, bf16[512,3456]{0,1:T(8,128)(2,1)} %constant_dynamic-update-slice_fusion, bf16[1152,3456]{1,0:T(8,128)(2,1)} %all-gather.6.cloned.1.call-done), kind=kOutput, calls=%fused_computation.53 | convolution fusion | flops 4078042624 | bytes 13872128 | tf_op jit(solution)/shard_map/dot_general | solution.py:29
  510.3 10.1 convolution_add_fusion
  522.4 9.9 all_to_all.29
  536.7 33.8 %reduce-scatter.7.cloned.1.call-done = bf16[72,2304]{1,0:T(8,128)(2,1)} async-done(((bf16[1152,2304]{1,0:T(8,128)(2,1)}), bf16[72,2304]{1,0:T(8,128)(2,1)}) %reduce-scatter.7.cloned.1.call-update) | async-done | bytes 331792 | tf_op jit(solution)/shard_map/reduce_scatter | solution.py:272
  570.5 81.2 %reduce-scatter.9.cloned.1.call-done = bf16[72,2304]{1,0:T(8,128)(2,1)} async-done(((bf16[1152,2304]{1,0:T(8,128)(2,1)}), bf16[72,2304]{1,0:T(8,128)(2,1)}) %reduce-scatter.9.cloned.1.call-update) | async-done | bytes 331792 | tf_op jit(solution)/shard_map/reduce_scatter | solution.py:272
  653.6 83.5 %reduce-scatter.15.cloned.1.call-done = bf16[288,576]{1,0:T(8,128)(2,1)} async-done(((bf16[4608,576]{1,0:T(8,128)(2,1)}), bf16[288,576]{1,0:T(8,128)(2,1)}) %reduce-scatter.15.cloned.1.call-update) | async-done | bytes 331792 | tf_op jit(solution)/shard_map/reduce_scatter | solution.py:272
  737.1 85.3 %reduce-scatter.17.cloned.1.call-done = bf16[288,576]{1,0:T(8,128)(2,1)} async-done(((bf16[4608,576]{1,0:T(8,128)(2,1)}), bf16[288,576]{1,0:T(8,128)(2,1)}) %reduce-scatter.17.cloned.1.call-update) | async-done | bytes 331792 | tf_op jit(solution)/shard_map/reduce_scatter | solution.py:272
  822.4 2.1 pad_maximum_fusion.2
  828.2 4.3 fusion.20
  832.5 4.9 all-reduce.11
  840.2 71.8 %all-reduce.16.cloned.1.call-done = bf16[32,1152]{1,0:T(8,128)(2,1)} async-done(((bf16[32,1152]{1,0:T(8,128)(2,1)}), bf16[32,1152]{1,0:T(8,128)(2,1)}) %all-reduce.16.cloned.1.call-update) | async-done | bytes 73744
  913.3 85.7 %all-reduce.18.cloned.1.call-done = (bf16[1152,432]{0,1:T(8,128)(2,1)}, bf16[72,3456]{1,0:T(8,128)(2,1)}, bf16[72,1152]{1,0:T(8,128)(2,1)}, bf16[72,4608]{1,0:T(8,128)(2,1)}, bf16[288,1152]{1,0:T(8,128)(2,1)}) async-done(((bf16[1152,432]{0,1:T(8,128)(2,1)}, bf16[72,3456]{1,0:T(8,128)(2,1)}, bf16[72,1152]{1,0:T(8,128)(2,1)}, bf16[72,4608]{1,0:T(8,128)(2,1)}, bf16[288,1152]{1,0:T(8,128)(2,1)}), ...) | async-done | bytes 2986000 | tf_op jit(solution)/shard_map/psum | solution.py:285
  999.0 2.7 convert_element_type.208
  (245 shorter events, 62.3 us)
Async XLA Ops:
  7.2 28.3 %copy-start = (bf16[1152,432]{0,1:T(8,128)(2,1)S(1)}, bf16[1152,432]{0,1:T(8,128)(2,1)}, u32[]{:S(2)}) copy-start(bf16[1152,432]{0,1:T(8,128)(2,1)} %param.17) | copy-start | bytes 2985988
  7.2 32.9 %copy-start.55 = (u32[32]{0:T(128)S(1)}, u32[32]{0:T(128)}, u32[]{:S(2)}) copy-start(u32[32]{0:T(128)} %constant.56) | copy-start | bytes 388
  7.2 36.1 %copy-start.57 = (bf16[72]{0:T(256)(128)(2,1)S(1)}, bf16[72]{0:T(256)(128)(2,1)}, u32[]{:S(2)}) copy-start(bf16[72]{0:T(256)(128)(2,1)} %param.22) | copy-start | bytes 436
  7.2 36.4 %copy-start.56 = (bf16[288]{0:T(512)(128)(2,1)S(1)}, bf16[288]{0:T(512)(128)(2,1)}, u32[]{:S(2)}) copy-start(bf16[288]{0:T(512)(128)(2,1)} %param.24) | copy-start | bytes 1732
  7.2 36.6 %copy-start.58 = (bf16[144]{0:T(256)(128)(2,1)S(1)}, bf16[144]{0:T(256)(128)(2,1)}, u32[]{:S(2)}) copy-start(bf16[144]{0:T(256)(128)(2,1)} %param.20) | copy-start | bytes 868
  7.2 101.9 %copy-start.2 = (bf16[2,256,1152]{2,1,0:T(8,128)(2,1)S(1)}, bf16[2,256,1152]{2,1,0:T(8,128)(2,1)}, u32[]{:S(2)}) copy-start(bf16[2,256,1152]{2,1,0:T(8,128)(2,1)} %param.14) | copy-start | bytes 3538948
  7.2 109.0 %all-gather.6.cloned.1.call-start = ((), (), s32[]{:S(2)}) async-start(), calls=%async_computation.8 | async-start | bytes 8460288 | tf_op jit(solution)/shard_map/all_gather | solution.py:94
  8.0 152.9 %all-gather.8.cloned.1.call-start = ((), (), s32[]{:S(2)}) async-start(), calls=%async_computation.9 | async-start | bytes 2820096 | tf_op jit(solution)/shard_map/all_gather | solution.py:96
  8.7 210.3 %all-gather.10.cloned.1.call-start = ((), (), s32[]{:S(2)}) async-start(), calls=%async_computation.10 | async-start | bytes 11280384 | tf_op jit(solution)/shard_map/all_gather | solution.py:98
  9.5 298.3 %all-gather.12.cloned.1.call-start = ((), (), s32[]{:S(2)}) async-start(), calls=%async_computation.11 | async-start | bytes 11280384 | tf_op jit(solution)/shard_map/all_gather | solution.py:100
  10.0 102.9 %copy-start.15 = (bf16[2,256,1152]{2,1,0:T(8,128)(2,1)S(1)}, bf16[2,256,1152]{2,1,0:T(8,128)(2,1)}, u32[]{:S(2)}) copy-start(bf16[2,256,1152]{2,1,0:T(8,128)(2,1)} %param.27) | copy-start | bytes 3538948
  34.8 80.9 %copy-start.34 = (bf16[32,1152]{1,0:T(8,128)(2,1)}, bf16[32,1152]{1,0:T(8,128)(2,1)S(1)}, u32[]{:S(2)}) copy-start(bf16[32,1152]{1,0:T(8,128)(2,1)S(1)} %reshape.206) | copy-start | bytes 221188
  36.5 75.6 %all-to-all-start = ((bf16[16,2,432]{2,1,0:T(2,128)(2,1)}), bf16[16,2,432]{2,1,0:T(2,128)(2,1)S(1)}, u32[]{:S(2)}, u32[]{:S(2)}) async-start(bf16[16,2,432]{2,1,0:T(2,128)(2,1)} %all_to_all.22), calls=%async_computation | async-start | bytes 65536 | tf_op jit(solution)/shard_map/all_to_all | solution.py:78
  40.0 494.7 %reduce-scatter.11.cloned.1.call-start = ((), (), s32[]{:S(2)}) async-start(), calls=%async_computation.14 | async-start | bytes 5640192 | tf_op jit(solution)/shard_map/reduce_scatter | solution.py:272
  109.4 6.8 copy-start.45
  112.4 3.3 copy-start.49
  116.2 8.9 copy-start.29
  143.5 7.9 copy-start.12
  151.4 4.6 copy-start.11
  160.8 4.1 copy-start.24
  160.9 4.1 copy-start.3
  166.7 52.3 %copy-start.51 = (f32[4608]{0:T(1024)S(1)}, f32[4608]{0:T(1024)}, u32[]{:S(2)}) copy-start(f32[4608]{0:T(1024)} %convert_element_type.192) | copy-start | bytes 55300
  307.8 18.1 %copy-start.32 = (bf16[2,256,1152]{2,1,0:T(8,128)(2,1)S(1)}, bf16[2,256,1152]{2,1,0:T(8,128)(2,1)}, u32[]{:S(2)}) copy-start(bf16[2,256,1152]{2,1,0:T(8,128)(2,1)} %add_convert_fusion.1) | copy-start | bytes 3538948
  331.0 203.7 %reduce-scatter.13.cloned.1.call-start = ((), (), s32[]{:S(2)}) async-start(), calls=%async_computation.15 | async-start | bytes 5640192 | tf_op jit(solution)/shard_map/reduce_scatter | solution.py:272
  338.4 232.0 %reduce-scatter.7.cloned.1.call-start = ((), (), s32[]{:S(2)}) async-start(), calls=%async_computation.12 | async-start | bytes 5640192 | tf_op jit(solution)/shard_map/reduce_scatter | solution.py:272
  352.3 3.5 copy-start.8
  352.3 3.8 copy-start.10
  352.3 4.1 copy-start.16
  352.3 4.1 copy-start.54
  379.5 4.8 copy-start.14
  396.5 255.1 %reduce-scatter.9.cloned.1.call-start = ((), (), s32[]{:S(2)}) async-start(), calls=%async_computation.13 | async-start | bytes 5640192 | tf_op jit(solution)/shard_map/reduce_scatter | solution.py:272
  410.0 327.1 %reduce-scatter.15.cloned.1.call-start = ((), (), s32[]{:S(2)}) async-start(), calls=%async_computation.16 | async-start | bytes 6266880 | tf_op jit(solution)/shard_map/reduce_scatter | solution.py:272
  419.0 403.4 %reduce-scatter.17.cloned.1.call-start = ((), (), s32[]{:S(2)}) async-start(), calls=%async_computation.17 | async-start | bytes 6266880 | tf_op jit(solution)/shard_map/reduce_scatter | solution.py:272
  428.7 483.3 %all-reduce.16.cloned.1.call-start = ((), (), s32[]{:S(2)}) async-start(), calls=%async_computation.18 | async-start | bytes 147456
  429.5 3.7 copy-start.23
  434.3 64.1 %copy-start.42 = (f32[2,1152]{1,0:T(2,128)S(1)}, f32[2,1152]{1,0:T(2,128)}, u32[]{:S(2)}) copy-start(f32[2,1152]{1,0:T(2,128)} %copy-done.41) | copy-start | bytes 27652
  498.4 10.4 %copy-start.4 = (bf16[2,256,1152]{2,1,0:T(8,128)(2,1)S(1)}, bf16[2,256,1152]{2,1,0:T(8,128)(2,1)}, u32[]{:S(2)}) copy-start(bf16[2,256,1152]{2,1,0:T(8,128)(2,1)} %param.14) | copy-start | bytes 3538948
  498.4 10.4 %copy-start.46 = (f32[2,256]{1,0:T(2,128)S(1)}, f32[2,256]{1,0:T(2,128)}, u32[]{:S(2)}) copy-start(f32[2,256]{1,0:T(2,128)} %copy-done.45) | copy-start | bytes 6148
  498.4 10.4 %copy-start.50 = (f32[2,256]{1,0:T(2,128)S(1)}, f32[2,256]{1,0:T(2,128)}, u32[]{:S(2)}) copy-start(f32[2,256]{1,0:T(2,128)} %add_rsqrt_fusion.1) | copy-start | bytes 6148
  510.3 10.1 copy-start.17
  510.3 10.1 copy-start.44
  520.4 11.9 %copy-start.35 = (bf16[32,1152]{1,0:T(8,128)(2,1)S(1)}, bf16[32,1152]{1,0:T(8,128)(2,1)}, u32[]{:S(2)}) copy-start(bf16[32,1152]{1,0:T(8,128)(2,1)} %copy-done.34) | copy-start | bytes 221188
  534.6 464.4 %all-reduce.18.cloned.1.call-start = ((), (), s32[]{:S(2)}) async-start(), calls=%async_computation.19 | async-start | bytes 5971968 | tf_op jit(solution)/shard_map/psum | solution.py:285
  651.7 172.9 %copy-start.33 = (bf16[72,2304]{1,0:T(8,128)(2,1)S(1)}, bf16[72,2304]{1,0:T(8,128)(2,1)}, u32[]{:S(2)}) copy-start(bf16[72,2304]{1,0:T(8,128)(2,1)} %reduce-scatter.9.cloned.1.call-done) | copy-start | bytes 995332
  653.6 174.6 %copy-start.5 = (bf16[2,256,1152]{2,1,0:T(8,128)(2,1)S(1)}, bf16[2,256,1152]{2,1,0:T(8,128)(2,1)}, u32[]{:S(2)}) copy-start(bf16[2,256,1152]{2,1,0:T(8,128)(2,1)} %param.14) | copy-start | bytes 3538948
  828.2 83.8 %copy-start.47 = (f32[2,1152]{1,0:T(2,128)S(1)}, f32[2,1152]{1,0:T(2,128)}, u32[]{:S(2)}) copy-start(f32[2,1152]{1,0:T(2,128)} %param.15) | copy-start | bytes 27652
  999.0 3.9 copy-start.36
  1001.7 3.3 copy-start.40
  (26 other events, 53.4 us)
Sparse Core Ops, SparseCore 0:
  10.2 75.2 all-gather.5
  87.7 41.8 all-gather.7
  131.9 87.1 all-gather.9
  221.2 86.5 all-gather.11
  331.1 76.3 reduce-scatter.10
  411.4 77.7 reduce-scatter.12
  493.3 77.1 reduce-scatter.6
  574.5 77.1 reduce-scatter.8
  655.6 81.4 reduce-scatter.14
  740.9 81.4 reduce-scatter.16
  825.9 86.0 all-reduce.15
  915.6 83.3 all-reduce.17
where the time goes:
time: 1020 us; the launch traced here: 1010 us
  waiting for transfers between devices  570 us (56%)
  blocking collectives  165 us (16%)
  matrix products  141 us (14%)
  local copies, waits for them, and re-layouts  60.7 us (6%)
  other arithmetic  51.8 us (5%)
  between operations  20.7 us (2%)
    reduce_scatter x6, waiting for transfers between devices, reduce_block(): lax.psum_scatter(block_term(factors, lax.axis_size('wide') * (rows // wid...  284 us
    unnamed x2, blocking collectives  126 us
    psum x1, waiting for transfers between devices, per_device(): lax.psum(grad_ada_weight.astype(jnp.bfloat16), 'narrow').astype(jnp.float32)  85.7 us
    all_gather x1, waiting for transfers between devices, per_device(): lax.all_gather(down_weight, 'wide', axis=0, tiled=True)  75.1 us
    unnamed x13, waiting for transfers between devices  74.6 us
    all_gather x1, waiting for transfers between devices, per_device(): lax.all_gather(up_weight, 'wide', axis=0, tiled=True)  50.5 us
    dot_general x5, matrix products, matmul_back(): lax.dot_general(left, right, (((1,), (1,)), ((), ())), preferred_element_...  43.9 us
    dot_general x8, matrix products, matmul_outer(): lax.dot_general(left, right, (((0,), (0,)), ((), ())), preferred_element_...  41.4 us
  transfers between devices with their start and end apart: 13, of which 8 were waited for; matrix products, arithmetic and copies ran while one was open for 21% of the time, Pallas kernels for 0%

commit v1 on v0

--- a/solution.py
+++ b/solution.py
@@ -90,12 +90,30 @@
         perceptron_scale,
         perceptron_gate,
     ) = segment_list
+
+    def return_all_the_widths(m):
+        shard_axis = "wide"
+        num = lax.axis_size(shard_axis)
+        by_rank = tuple(((k0, (k0 + 1) % num) for k0 in range(num)))
+        views = tuple(((k0, (k0 - 1) % num) for k0 in range(num)))
+        w1, row_out = ([m], [m])
+        for _ in range(num // 2):
+            w1.append(lax.ppermute(w1[-1], axis_name=shard_axis, perm=by_rank))
+        for _ in range((num - 1) // 2):
+            row_out.append(lax.ppermute(row_out[-1], perm=views, axis_name=shard_axis))
+        block_next = jnp.roll(
+            jnp.concatenate([*w1[::-1], *row_out[1:]], axis=0),
+            (lax.axis_index(shard_axis) - num // 2) * m.shape[0],
+            axis=0,
+        )
+        return block_next
+
     fetched = (
         lax.all_gather(inproj_weight, "wide", axis=0, tiled=True),
         lax.all_gather(inproj_bias, "wide", axis=0, tiled=True),
         lax.all_gather(outproj_weight, "wide", axis=0, tiled=True),
         lax.all_gather(outproj_bias, "wide", axis=0, tiled=True),
-        lax.all_gather(up_weight, "wide", axis=0, tiled=True),
+        return_all_the_widths(up_weight),
         lax.all_gather(up_bias, "wide", axis=0, tiled=True),
         lax.all_gather(down_weight, "wide", axis=0, tiled=True),
         lax.all_gather(down_bias, "wide", axis=0, tiled=True),

time: 1020 us -> 1080 us (1.059)
  local copies, waits for them, and re-layouts: 60.7 us -> 112 us
  waiting for transfers between devices: 570 us -> 523 us
  starting transfers between devices: 4.45 us -> 39.7 us
  blocking collectives: 165 us -> 190 us
    ppermute x0 -> x15, waiting for transfers between devices: none -> 90.8 us  [the longest x8 63.4 us: return_all_the_widths(): w1.append(lax.ppermute(w1[-1], axis_name=shard_axis, perm=by_rank))]
    all_gather x1, waiting for transfers between devices: 75.1 us -> 0.02 us  [per_device(): lax.all_gather(down_weight, 'wide', axis=0, tiled=True)]
    all_gather x1, waiting for transfers between devices: 50.5 us -> 0.02 us  [per_device(): lax.all_gather(up_weight, 'wide', axis=0, tiled=True)]
    unnamed x147 -> x198, local copies, waits for them, and re-layouts: 17.1 us -> 66.4 us
    ppermute x0 -> x15, starting transfers between devices: none -> 35.5 us  [the longest x7 27.3 us: return_all_the_widths(): row_out.append(lax.ppermute(row_out[-1], perm=views, axis_name=shard_axis))]
    unnamed x2, blocking collectives: 126 us -> 144 us
  transfers between devices with their start and end apart: 13 -> 28, of which waited for: 8 -> 13; matrix products, arithmetic and copies ran while one was open for 21% -> 26% of each run, Pallas kernels for 0% -> 0%
where the time goes in v1:
time: 1080 us
  waiting for transfers between devices  523 us (48%)
  blocking collectives  190 us (18%)
  matrix products  139 us (13%)
  local copies, waits for them, and re-layouts  112 us (10%)
  other arithmetic  51.6 us (5%)
  starting transfers between devices  39.7 us (4%)
  between operations  20.7 us (2%)
    reduce_scatter x6, waiting for transfers between devices, reduce_block(): lax.psum_scatter(block_term(factors, lax.axis_size('wide') * (rows // wid...  273 us
    unnamed x2, blocking collectives  144 us
    psum x1, waiting for transfers between devices, per_device(): lax.psum(grad_ada_weight.astype(jnp.bfloat16), 'narrow').astype(jnp.float32)  85.7 us
    unnamed x13, waiting for transfers between devices  73.7 us
    unnamed x198, local copies, waits for them, and re-layouts  66.4 us
    ppermute x8, waiting for transfers between devices, return_all_the_widths(): w1.append(lax.ppermute(w1[-1], axis_name=shard_axis, perm=by_rank))  63.4 us
    dot_general x5, matrix products, matmul_back(): lax.dot_general(left, right, (((1,), (1,)), ((), ())), preferred_element_...  42.9 us
    dot_general x5, matrix products, matmul_rows(): return jnp.dot(left, right, preferred_element_type=jnp.float32)  39.9 us
  transfers between devices with their start and end apart: 28, of which 13 were waited for; matrix products, arithmetic and copies ran while one was open for 26% of the time, Pallas kernels for 0%

profile of v1, /device:TPU:0, one launch (start us, length us, event | category | flops | bytes accessed | tf_op | source)
XLA Modules:
  0.0 1076.8 jit_solution(8513776396981056455)
XLA Ops:
  10.0 13.6 %collective-permute-done = bf16[72,4608]{1,0:T(8,128)(2,1)S(1)} collective-permute-done((bf16[72,4608]{1,0:T(8,128)(2,1)}, bf16[72,4608]{1,0:T(8,128)(2,1)S(1)}, u32[]{:S(2)}, u32[]{:S(2)}) %collective-permute-start) | collective-permute-done | bytes 663584 | tf_op jit(solution)/shard_map/ppermute | solution.py:101
  24.4 4.4 collective-permute-start.8
  28.9 21.1 %collective-permute-done.1 = bf16[72,4608]{1,0:T(8,128)(2,1)S(1)} collective-permute-done((bf16[72,4608]{1,0:T(8,128)(2,1)S(1)}, bf16[72,4608]{1,0:T(8,128)(2,1)S(1)}, u32[]{:S(2)}, u32[]{:S(2)}) %collective-permute-start.1) | collective-permute-done | bytes 663584 | tf_op jit(solution)/shard_map/ppermute | solution.py:101
  50.8 4.4 collective-permute-start.9
  55.3 19.6 %collective-permute-done.2 = bf16[72,4608]{1,0:T(8,128)(2,1)S(1)} collective-permute-done((bf16[72,4608]{1,0:T(8,128)(2,1)S(1)}, bf16[72,4608]{1,0:T(8,128)(2,1)S(1)}, u32[]{:S(2)}, u32[]{:S(2)}) %collective-permute-start.2) | collective-permute-done | bytes 663584 | tf_op jit(solution)/shard_map/ppermute | solution.py:101
  75.7 4.4 collective-permute-start.10
  80.1 9.1 collective-permute-done.3
  89.2 31.1 %all-gather = bf16[16,2,1152]{2,1,0:T(2,128)(2,1)S(1)} all-gather(bf16[1,2,1152]{2,1,0:T(2,128)(2,1)S(1)} %fusion.44), channel_id=1, replica_groups=mesh['narrow'=2,'wide'=16] {'wide'}, dimensions={0}, use_global_device_ids=true | all-gather | bytes 78336 | tf_op jit(solution)/shard_map/all_gather | solution.py:74
  122.1 3.5 all-to-all-start
  129.5 63.6 %all-reduce.10 = (bf16[2304]{0:T(1024)(128)(2,1)S(1)}, bf16[1152]{0:T(1024)(128)(2,1)S(1)}, bf16[4608]{0:T(1024)(128)(2,1)S(1)}) all-reduce(bf16[2304]{0:T(1024)(128)(2,1)S(1)} %dynamic-update-slice, bf16[1152]{0:T(1024)(128)(2,1)S(1)} %dynamic-update-slice.1, ...), channel_id=1, replica_groups=mesh['narrow'=2,'wide'=16] {'wide'}, use_global_device_ids=true, to_apply=%add | all-reduce | flops 8064 | bytes 32256
  197.9 4.4 collective-permute-done.11
  202.4 4.6 collective-permute-start.12
  209.8 19.9 %collective-permute-done.12 = bf16[72,4608]{1,0:T(8,128)(2,1)} collective-permute-done((bf16[72,4608]{1,0:T(8,128)(2,1)}, bf16[72,4608]{1,0:T(8,128)(2,1)}, u32[]{:S(2)}, u32[]{:S(2)}) %collective-permute-start.12) | collective-permute-done | bytes 663584 | tf_op jit(solution)/shard_map/ppermute | solution.py:103
  229.7 4.6 collective-permute-start.13
  234.3 5.1 collective-permute-start.7
  246.4 4.8 collective-permute-start.14
  297.7 8.8 add_convert_fusion
  308.5 5.0 reshape.221
  316.1 5.8 reshape.222
  324.9 4.7 reshape.220
  329.6 3.6 copy.95
  342.6 4.1 convolution_add_fusion.1
  349.1 16.6 %multiply_convert_fusion = (bf16[512,4608]{1,0:T(8,128)(2,1)S(1)}, f32[512,4608]{1,0:T(8,128)}) fusion(f32[4608]{0:T(1024)S(1)} %copy-done.60, bf16[512,1152]{1,0:T(8,128)(2,1)S(1)} %bitcast.130, bf16[2304,4608]{1,0:T(8,128)(2,1)} %constant_dynamic-update-slice_fusion, s32[]{:T(128)S(6)} %select_n.26), kind=kOutput, calls=%fused_computation.14 | convolution fusion | flops 5459410944 | bytes 25970692 | tf_op jit(solution)/shard_map/dot_general | solution.py:25
  367.8 5.7 convolution_convert_fusion.4
  373.6 8.9 convolution_convert_fusion.3
  382.6 16.0 %fusion.50 = (bf16[4608]{0:T(1024)(128)(2,1)S(1)}, bf16[512,4608]{1,0:T(8,128)(2,1)S(1)}) fusion(f32[512,4608]{1,0:T(8,128)} %get-tuple-element.67, f32[4608]{0:T(1024)S(1)} %copy-done.60, bf16[512,1152]{1,0:T(8,128)(2,1)} %bitcast.125, bf16[4608,1152]{1,0:T(8,128)(2,1)} %all-gather.10.cloned.1.call-done), kind=kOutput, calls=%fused_computation.159 | convolution fusion | flops 5487717888 | bytes 25979904 | tf_op jit(solution)/shard_map/dot_general | solution.py:29
  400.7 5.1 convolution_convert_fusion.1
  405.9 7.6 convolution_convert_fusion
  413.5 12.8 %fusion.31 = (f32[512]{0:T(512)S(1)}, f32[512,1152]{1,0:T(8,128)}) fusion(f32[2,1152]{1,0:T(2,128)S(1)} %get-tuple-element.52, bf16[512,4608]{1,0:T(8,128)(2,1)} %copy-done.69, bf16[1152,4608]{1,0:T(8,128)(2,1)} %all-gather.12.cloned.1.call-done), kind=kOutput, calls=%fused_computation.58 | convolution fusion | flops 5436997120 | bytes 17705984 | tf_op jit(solution)/shard_map/dot_general | solution.py:29
  426.3 3.4 fusion.32
  437.4 5.7 reshape.223
  443.1 4.2 copy.99
  447.2 6.3 multiply_reduce_fusion
  453.5 4.7 multiply_convert_fusion.1
  464.5 6.0 convolution_convert_fusion.2
  470.8 5.4 fusion.34
  492.6 80.7 %all-reduce.9 = (bf16[1152]{0:T(1024)(128)(2,1)S(1)}, bf16[2304]{0:T(1024)(128)(2,1)S(1)}, bf16[1152]{0:T(1024)(128)(2,1)S(1)}, bf16[4608]{0:T(1024)(128)(2,1)S(1)}, bf16[1152]{0:T(1024)(128)(2,1)S(1)}) all-reduce(bf16[1152]{0:T(1024)(128)(2,1)S(1)} %dynamic-update-slice.3, ...), channel_id=1, replica_groups=mesh['narrow'=2,'wide'=16] {'wide'}, use_global_device_ids=true, to_apply=%add.3 | all-reduce | flops 10368 | bytes 41472
  573.3 10.4 fusion.30
  585.2 10.0 convolution_add_fusion
  597.2 9.5 all_to_all.29
  611.3 31.7 %reduce-scatter.11.cloned.1.call-done = bf16[72,2304]{1,0:T(8,128)(2,1)} async-done(((bf16[1152,2304]{1,0:T(8,128)(2,1)}), bf16[72,2304]{1,0:T(8,128)(2,1)}) %reduce-scatter.11.cloned.1.call-update) | async-done | bytes 331792 | tf_op jit(solution)/shard_map/reduce_scatter | solution.py:290
  643.0 81.2 %reduce-scatter.13.cloned.1.call-done = bf16[72,2304]{1,0:T(8,128)(2,1)} async-done(((bf16[1152,2304]{1,0:T(8,128)(2,1)}), bf16[72,2304]{1,0:T(8,128)(2,1)}) %reduce-scatter.13.cloned.1.call-update) | async-done | bytes 331792 | tf_op jit(solution)/shard_map/reduce_scatter | solution.py:290
  726.2 79.2 %reduce-scatter.7.cloned.1.call-done = bf16[72,2304]{1,0:T(8,128)(2,1)} async-done(((bf16[1152,2304]{1,0:T(8,128)(2,1)}), bf16[72,2304]{1,0:T(8,128)(2,1)}) %reduce-scatter.7.cloned.1.call-update) | async-done | bytes 331792 | tf_op jit(solution)/shard_map/reduce_scatter | solution.py:290
  805.4 81.0 %reduce-scatter.9.cloned.1.call-done = bf16[72,2304]{1,0:T(8,128)(2,1)} async-done(((bf16[1152,2304]{1,0:T(8,128)(2,1)}), bf16[72,2304]{1,0:T(8,128)(2,1)}) %reduce-scatter.9.cloned.1.call-update) | async-done | bytes 331792 | tf_op jit(solution)/shard_map/reduce_scatter | solution.py:290
  892.9 4.3 fusion.22
  897.2 4.9 all-reduce.11
  904.9 71.0 %all-reduce.16.cloned.1.call-done = bf16[32,1152]{1,0:T(8,128)(2,1)} async-done(((bf16[32,1152]{1,0:T(8,128)(2,1)}), bf16[32,1152]{1,0:T(8,128)(2,1)}) %all-reduce.16.cloned.1.call-update) | async-done | bytes 73744
  977.2 85.7 %all-reduce.18.cloned.1.call-done = (bf16[1152,432]{0,1:T(8,128)(2,1)}, bf16[72,3456]{1,0:T(8,128)(2,1)}, bf16[72,1152]{1,0:T(8,128)(2,1)}, bf16[72,4608]{1,0:T(8,128)(2,1)}, bf16[288,1152]{1,0:T(8,128)(2,1)}) async-done(((bf16[1152,432]{0,1:T(8,128)(2,1)}, bf16[72,3456]{1,0:T(8,128)(2,1)}, bf16[72,1152]{1,0:T(8,128)(2,1)}, bf16[72,4608]{1,0:T(8,128)(2,1)}, bf16[288,1152]{1,0:T(8,128)(2,1)}), ...) | async-done | bytes 2986000 | tf_op jit(solution)/shard_map/psum | solution.py:303
  (327 shorter events, 148.2 us)
Async XLA Ops:
  7.2 113.8 %copy-start = (bf16[1152,432]{0,1:T(8,128)(2,1)S(1)}, bf16[1152,432]{0,1:T(8,128)(2,1)}, u32[]{:S(2)}) copy-start(bf16[1152,432]{0,1:T(8,128)(2,1)} %param.17) | copy-start | bytes 2985988
  7.2 119.0 %copy-start.64 = (u32[32]{0:T(128)S(1)}, u32[32]{0:T(128)}, u32[]{:S(2)}) copy-start(u32[32]{0:T(128)} %constant.84) | copy-start | bytes 388
  7.2 121.5 %copy-start.66 = (bf16[72]{0:T(256)(128)(2,1)S(1)}, bf16[72]{0:T(256)(128)(2,1)}, u32[]{:S(2)}) copy-start(bf16[72]{0:T(256)(128)(2,1)} %param.22) | copy-start | bytes 436
  7.2 121.8 %copy-start.65 = (bf16[288]{0:T(512)(128)(2,1)S(1)}, bf16[288]{0:T(512)(128)(2,1)}, u32[]{:S(2)}) copy-start(bf16[288]{0:T(512)(128)(2,1)} %param.24) | copy-start | bytes 1732
  7.2 122.0 %copy-start.67 = (bf16[144]{0:T(256)(128)(2,1)S(1)}, bf16[144]{0:T(256)(128)(2,1)}, u32[]{:S(2)}) copy-start(bf16[144]{0:T(256)(128)(2,1)} %param.20) | copy-start | bytes 868
  7.2 185.9 %copy-start.2 = (bf16[2,256,1152]{2,1,0:T(8,128)(2,1)S(1)}, bf16[2,256,1152]{2,1,0:T(8,128)(2,1)}, u32[]{:S(2)}) copy-start(bf16[2,256,1152]{2,1,0:T(8,128)(2,1)} %param.14) | copy-start | bytes 3538948
  7.2 290.5 %all-gather.6.cloned.1.call-start = ((), (), s32[]{:S(2)}) async-start(), calls=%async_computation.8 | async-start | bytes 8460288 | tf_op jit(solution)/shard_map/all_gather | solution.py:112
  8.0 334.6 %all-gather.8.cloned.1.call-start = ((), (), s32[]{:S(2)}) async-start(), calls=%async_computation.9 | async-start | bytes 2820096 | tf_op jit(solution)/shard_map/all_gather | solution.py:114
  8.7 373.9 %all-gather.10.cloned.1.call-start = ((), (), s32[]{:S(2)}) async-start(), calls=%async_computation.10 | async-start | bytes 11280384 | tf_op jit(solution)/shard_map/all_gather | solution.py:118
  9.5 230.0 %copy-start.15 = (bf16[2,256,1152]{2,1,0:T(8,128)(2,1)S(1)}, bf16[2,256,1152]{2,1,0:T(8,128)(2,1)}, u32[]{:S(2)}) copy-start(bf16[2,256,1152]{2,1,0:T(8,128)(2,1)} %param.27) | copy-start | bytes 3538948
  9.5 14.1 %collective-permute-start = (bf16[72,4608]{1,0:T(8,128)(2,1)}, bf16[72,4608]{1,0:T(8,128)(2,1)S(1)}, u32[]{:S(2)}, u32[]{:S(2)}) collective-permute-start(bf16[72,4608]{1,0:T(8,128)(2,1)} %param.23), channel_id=1, source_target_pairs={{0,1},{1,2},{2,3},{3,4},{4,5},{5,6},{6,7},{7,8},{8,9},{9,10},{10,1... | collective-permute-start | bytes 1990664 | tf_op jit(solution)/shard_map/ppermute | solution.py:101
  24.4 25.5 %collective-permute-start.1 = (bf16[72,4608]{1,0:T(8,128)(2,1)S(1)}, bf16[72,4608]{1,0:T(8,128)(2,1)S(1)}, u32[]{:S(2)}, u32[]{:S(2)}) collective-permute-start(bf16[72,4608]{1,0:T(8,128)(2,1)S(1)} %collective-permute-done), channel_id=1, source_target_pairs={{0,1},{1,2},{2,3},{3,4},{4,5},{5,6},{6,7},{7,8},{8,9},{9,10},{10,1... | collective-permute-start | bytes 1990664 | tf_op jit(solution)/shard_map/ppermute | solution.py:101
  24.4 25.6 %collective-permute-start.8 = (bf16[72,4608]{1,0:T(8,128)(2,1)}, bf16[72,4608]{1,0:T(8,128)(2,1)S(1)}, u32[]{:S(2)}, u32[]{:S(2)}) collective-permute-start(bf16[72,4608]{1,0:T(8,128)(2,1)} %param.23), channel_id=1, source_target_pairs={{0,15},{1,0},{2,1},{3,2},{4,3},{5,4},{6,5},{7,6},{8,7},{9,8},{10,9... | collective-permute-start | bytes 1990664 | tf_op jit(solution)/shard_map/ppermute | solution.py:103
  50.0 24.9 %collective-permute-start.2 = (bf16[72,4608]{1,0:T(8,128)(2,1)S(1)}, bf16[72,4608]{1,0:T(8,128)(2,1)S(1)}, u32[]{:S(2)}, u32[]{:S(2)}) collective-permute-start(bf16[72,4608]{1,0:T(8,128)(2,1)S(1)} %collective-permute-done.1), channel_id=1, source_target_pairs={{0,1},{1,2},{2,3},{3,4},{4,5},{5,6},{6,7},{7,8},{8,9},{9,10},{10,1... | collective-permute-start | bytes 1990664 | tf_op jit(solution)/shard_map/ppermute | solution.py:101
  50.8 24.7 %collective-permute-start.9 = (bf16[72,4608]{1,0:T(8,128)(2,1)S(1)}, bf16[72,4608]{1,0:T(8,128)(2,1)}, u32[]{:S(2)}, u32[]{:S(2)}) collective-permute-start(bf16[72,4608]{1,0:T(8,128)(2,1)S(1)} %collective-permute-done.8), channel_id=1, source_target_pairs={{0,15},{1,0},{2,1},{3,2},{4,3},{5,4},{6,5},{7,6},{8,7},{9,8},{10,9... | collective-permute-start | bytes 1990664 | tf_op jit(solution)/shard_map/ppermute | solution.py:103
  74.9 14.3 %collective-permute-start.3 = (bf16[72,4608]{1,0:T(8,128)(2,1)S(1)}, bf16[72,4608]{1,0:T(8,128)(2,1)}, u32[]{:S(2)}, u32[]{:S(2)}) collective-permute-start(bf16[72,4608]{1,0:T(8,128)(2,1)S(1)} %collective-permute-done.2), channel_id=1, source_target_pairs={{0,1},{1,2},{2,3},{3,4},{4,5},{5,6},{6,7},{7,8},{8,9},{9,10},{10,1... | collective-permute-start | bytes 1990664 | tf_op jit(solution)/shard_map/ppermute | solution.py:101
  75.7 117.6 %collective-permute-start.10 = (bf16[72,4608]{1,0:T(8,128)(2,1)}, bf16[72,4608]{1,0:T(8,128)(2,1)}, u32[]{:S(2)}, u32[]{:S(2)}) collective-permute-start(bf16[72,4608]{1,0:T(8,128)(2,1)} %collective-permute-done.9), channel_id=1, source_target_pairs={{0,15},{1,0},{2,1},{3,2},{4,3},{5,4},{6,5},{7,6},{8,7},{9,8},{10,9... | collective-permute-start | bytes 1990664 | tf_op jit(solution)/shard_map/ppermute | solution.py:103
  89.2 104.2 %collective-permute-start.4 = (bf16[72,4608]{1,0:T(8,128)(2,1)}, bf16[72,4608]{1,0:T(8,128)(2,1)}, u32[]{:S(2)}, u32[]{:S(2)}) collective-permute-start(bf16[72,4608]{1,0:T(8,128)(2,1)} %collective-permute-done.3), channel_id=1, source_target_pairs={{0,1},{1,2},{2,3},{3,4},{4,5},{5,6},{6,7},{7,8},{8,9},{9,10},{10,1... | collective-permute-start | bytes 1990664 | tf_op jit(solution)/shard_map/ppermute | solution.py:101
  120.3 121.8 %copy-start.44 = (bf16[32,1152]{1,0:T(8,128)(2,1)}, bf16[32,1152]{1,0:T(8,128)(2,1)S(1)}, u32[]{:S(2)}) copy-start(bf16[32,1152]{1,0:T(8,128)(2,1)S(1)} %reshape.206) | copy-start | bytes 221188
  122.1 86.9 %all-to-all-start = ((bf16[16,2,432]{2,1,0:T(2,128)(2,1)}), bf16[16,2,432]{2,1,0:T(2,128)(2,1)S(1)}, u32[]{:S(2)}, u32[]{:S(2)}) async-start(bf16[16,2,432]{2,1,0:T(2,128)(2,1)} %all_to_all.22), calls=%async_computation | async-start | bytes 65536 | tf_op jit(solution)/shard_map/all_to_all | solution.py:78
  125.6 288.0 %all-gather.12.cloned.1.call-start = ((), (), s32[]{:S(2)}) async-start(), calls=%async_computation.11 | async-start | bytes 11280384 | tf_op jit(solution)/shard_map/all_gather | solution.py:167
  126.1 483.0 %reduce-scatter.15.cloned.1.call-start = ((), (), s32[]{:S(2)}) async-start(), calls=%async_computation.16 | async-start | bytes 6266880 | tf_op jit(solution)/shard_map/reduce_scatter | solution.py:290
  193.3 9.0 collective-permute-start.11
  193.4 13.5 %collective-permute-start.5 = (bf16[72,4608]{1,0:T(8,128)(2,1)}, bf16[72,4608]{1,0:T(8,128)(2,1)}, u32[]{:S(2)}, u32[]{:S(2)}) collective-permute-start(bf16[72,4608]{1,0:T(8,128)(2,1)} %collective-permute-done.4), channel_id=1, source_target_pairs={{0,1},{1,2},{2,3},{3,4},{4,5},{5,6},{6,7},{7,8},{8,9},{9,10},{10,1... | collective-permute-start | bytes 1990664 | tf_op jit(solution)/shard_map/ppermute | solution.py:101
  193.9 49.4 %copy-start.55 = (f32[2,256]{1,0:T(2,128)}, f32[2,256]{1,0:T(2,128)S(1)}, u32[]{:S(2)}) copy-start(f32[2,256]{1,0:T(2,128)S(1)} %broadcast_multiply_fusion.5) | copy-start | bytes 6148
  202.4 27.4 %collective-permute-start.12 = (bf16[72,4608]{1,0:T(8,128)(2,1)}, bf16[72,4608]{1,0:T(8,128)(2,1)}, u32[]{:S(2)}, u32[]{:S(2)}) collective-permute-start(bf16[72,4608]{1,0:T(8,128)(2,1)} %collective-permute-done.11), channel_id=1, source_target_pairs={{0,15},{1,0},{2,1},{3,2},{4,3},{5,4},{6,5},{7,6},{8,7},{9,8},{10,9... | collective-permute-start | bytes 1990664 | tf_op jit(solution)/shard_map/ppermute | solution.py:103
  207.0 27.4 %collective-permute-start.6 = (bf16[72,4608]{1,0:T(8,128)(2,1)}, bf16[72,4608]{1,0:T(8,128)(2,1)}, u32[]{:S(2)}, u32[]{:S(2)}) collective-permute-start(bf16[72,4608]{1,0:T(8,128)(2,1)} %collective-permute-done.5), channel_id=1, source_target_pairs={{0,1},{1,2},{2,3},{3,4},{4,5},{5,6},{6,7},{7,8},{8,9},{9,10},{10,1... | collective-permute-start | bytes 1990664 | tf_op jit(solution)/shard_map/ppermute | solution.py:101
  209.8 42.3 %copy-start.51 = (f32[2,1152]{1,0:T(2,128)}, f32[2,1152]{1,0:T(2,128)S(1)}, u32[]{:S(2)}) copy-start(f32[2,1152]{1,0:T(2,128)S(1)} %get-tuple-element.54) | copy-start | bytes 27652
  209.8 42.3 %copy-start.53 = (f32[2,1152]{1,0:T(2,128)}, f32[2,1152]{1,0:T(2,128)S(1)}, u32[]{:S(2)}) copy-start(f32[2,1152]{1,0:T(2,128)S(1)} %get-tuple-element.50) | copy-start | bytes 27652
  229.7 16.7 %collective-permute-start.13 = (bf16[72,4608]{1,0:T(8,128)(2,1)}, bf16[72,4608]{1,0:T(8,128)(2,1)S(1)}, u32[]{:S(2)}, u32[]{:S(2)}) collective-permute-start(bf16[72,4608]{1,0:T(8,128)(2,1)} %collective-permute-done.12), channel_id=1, source_target_pairs={{0,15},{1,0},{2,1},{3,2},{4,3},{5,4},{6,5},{7,6},{8,7},{9,8},{10,9... | collective-permute-start | bytes 1990664 | tf_op jit(solution)/shard_map/ppermute | solution.py:103
  234.3 16.9 %collective-permute-start.7 = (bf16[72,4608]{1,0:T(8,128)(2,1)}, bf16[72,4608]{1,0:T(8,128)(2,1)S(1)}, u32[]{:S(2)}, u32[]{:S(2)}) collective-permute-start(bf16[72,4608]{1,0:T(8,128)(2,1)} %collective-permute-done.6), channel_id=1, source_target_pairs={{0,1},{1,2},{2,3},{3,4},{4,5},{5,6},{6,7},{7,8},{8,9},{9,10},{10,1... | collective-permute-start | bytes 1990664 | tf_op jit(solution)/shard_map/ppermute | solution.py:101
  243.3 54.4 %copy-start.39 = (bf16[2,256,1152]{2,1,0:T(8,128)(2,1)}, bf16[2,256,1152]{2,1,0:T(8,128)(2,1)S(1)}, u32[]{:S(2)}) copy-start(bf16[2,256,1152]{2,1,0:T(8,128)(2,1)S(1)} %fusion.17) | copy-start | bytes 3538948
  246.4 27.3 %collective-permute-start.14 = (bf16[72,4608]{1,0:T(8,128)(2,1)S(1)}, bf16[72,4608]{1,0:T(8,128)(2,1)S(1)}, u32[]{:S(2)}, u32[]{:S(2)}) collective-permute-start(bf16[72,4608]{1,0:T(8,128)(2,1)S(1)} %collective-permute-done.13), channel_id=1, source_target_pairs={{0,15},{1,0},{2,1},{3,2},{4,3},{5,4},{6,5},{7,6},{8,7},{9,8},{10,9... | collective-permute-start | bytes 1990664 | tf_op jit(solution)/shard_map/ppermute | solution.py:103
  349.0 16.7 %copy-start.42 = (bf16[2,256,1152]{2,1,0:T(8,128)(2,1)}, bf16[2,256,1152]{2,1,0:T(8,128)(2,1)S(1)}, u32[]{:S(2)}) copy-start(bf16[2,256,1152]{2,1,0:T(8,128)(2,1)S(1)} %add_convert_fusion.1) | copy-start | bytes 3538948
  349.0 18.8 %copy-start.38 = (bf16[2,256,1152]{2,1,0:T(8,128)(2,1)S(1)}, bf16[2,256,1152]{2,1,0:T(8,128)(2,1)}, u32[]{:S(2)}) copy-start(bf16[2,256,1152]{2,1,0:T(8,128)(2,1)} %get-tuple-element.40) | copy-start | bytes 3538948
  373.6 235.6 %reduce-scatter.17.cloned.1.call-start = ((), (), s32[]{:S(2)}) async-start(), calls=%async_computation.17 | async-start | bytes 6266880 | tf_op jit(solution)/shard_map/reduce_scatter | solution.py:290
  382.6 260.5 %reduce-scatter.11.cloned.1.call-start = ((), (), s32[]{:S(2)}) async-start(), calls=%async_computation.14 | async-start | bytes 5640192 | tf_op jit(solution)/shard_map/reduce_scatter | solution.py:290
  382.6 18.1 %copy-start.43 = (bf16[2,256,1152]{2,1,0:T(8,128)(2,1)S(1)}, bf16[2,256,1152]{2,1,0:T(8,128)(2,1)}, u32[]{:S(2)}) copy-start(bf16[2,256,1152]{2,1,0:T(8,128)(2,1)} %copy-done.42) | copy-start | bytes 3538948
  405.8 318.4 %reduce-scatter.13.cloned.1.call-start = ((), (), s32[]{:S(2)}) async-start(), calls=%async_computation.15 | async-start | bytes 5640192 | tf_op jit(solution)/shard_map/reduce_scatter | solution.py:290
  413.5 392.0 %reduce-scatter.7.cloned.1.call-start = ((), (), s32[]{:S(2)}) async-start(), calls=%async_computation.12 | async-start | bytes 5640192 | tf_op jit(solution)/shard_map/reduce_scatter | solution.py:290
  470.5 415.9 %reduce-scatter.9.cloned.1.call-start = ((), (), s32[]{:S(2)}) async-start(), calls=%async_computation.13 | async-start | bytes 5640192 | tf_op jit(solution)/shard_map/reduce_scatter | solution.py:290
  484.0 491.8 %all-reduce.16.cloned.1.call-start = ((), (), s32[]{:S(2)}) async-start(), calls=%async_computation.18 | async-start | bytes 147456
  488.7 84.6 %copy-start.52 = (f32[2,1152]{1,0:T(2,128)S(1)}, f32[2,1152]{1,0:T(2,128)}, u32[]{:S(2)}) copy-start(f32[2,1152]{1,0:T(2,128)} %copy-done.51) | copy-start | bytes 27652
  573.3 10.4 copy-start.59
  595.2 11.5 %copy-start.45 = (bf16[32,1152]{1,0:T(8,128)(2,1)S(1)}, bf16[32,1152]{1,0:T(8,128)(2,1)}, u32[]{:S(2)}) copy-start(bf16[32,1152]{1,0:T(8,128)(2,1)} %copy-done.44) | copy-start | bytes 221188
  609.1 453.7 %all-reduce.18.cloned.1.call-start = ((), (), s32[]{:S(2)}) async-start(), calls=%async_computation.19 | async-start | bytes 5971968 | tf_op jit(solution)/shard_map/psum | solution.py:303
  611.3 281.5 %copy-start.5 = (bf16[2,256,1152]{2,1,0:T(8,128)(2,1)S(1)}, bf16[2,256,1152]{2,1,0:T(8,128)(2,1)}, u32[]{:S(2)}) copy-start(bf16[2,256,1152]{2,1,0:T(8,128)(2,1)} %param.14) | copy-start | bytes 3538948
  892.9 83.0 %copy-start.57 = (f32[2,1152]{1,0:T(2,128)S(1)}, f32[2,1152]{1,0:T(2,128)}, u32[]{:S(2)}) copy-start(f32[2,1152]{1,0:T(2,128)} %param.15) | copy-start | bytes 27652
  (51 other events, 191.4 us)
Sparse Core Ops, SparseCore 0:
  10.2 108.7 all-gather.5
  121.2 41.8 all-gather.7
  165.4 115.8 all-gather.9
  283.4 95.3 all-gather.11
  382.6 92.6 reduce-scatter.14
  479.1 82.2 reduce-scatter.16
  565.5 77.5 reduce-scatter.10
  647.1 77.1 reduce-scatter.12
  728.3 77.0 reduce-scatter.6
  809.3 77.0 reduce-scatter.8
  889.9 85.8 all-reduce.15
  979.4 83.3 all-reduce.17
